TPU v7x, 256 devices: a whole 4x4x8 slice. The times are simulated.
256 devices in a mesh: row: 16 (over x_lo, y, core), col: 16 (over z, x_hi).
Axes of the slice: x: 4 (x_hi: 2, x_lo: 2; x = x_hi * 2 + x_lo), y: 4, z: 8, core: 2. Of those that a mesh axis runs over, the one named last changes fastest.
Arguments:
- adj_values: bfloat16 [2, 16, 16, 20, 128, 128], P(None, 'row', 'col'), may hold values from -6 to 6
- block_rows: int32 [2, 16, 16, 20], P(None, 'row', 'col'), may hold values from 0 to 47, as said below
- block_cols: int32 [2, 16, 16, 20], P(None, 'row', 'col'), may hold values from 0 to 15, as said below
- block_counts: int32 [2, 16, 16], P(None, 'row', 'col'), may hold values from 5 to 20, as said below
- block_scales: bfloat16 [2, 16, 16, 20], P(None, 'row', 'col'), may hold values from 0.0049743652 to 0.049804688
- panel_features: bfloat16 [2, 256, 32768], P(None, 'col', 'row'), may hold values from -6 to 6
- weight: bfloat16 [256, 256], replicated, may hold values from -0.375 to 0.375
- out_bias: float32 [256], replicated, may hold values from -3 to 3
Outputs:
- layer_out: bfloat16 [98304, 256], P(('row', 'col'))
Inputs may be any that keep to these rules, and one draw needn't show every extreme that they name: `block_rows`: block rows are local to the 48 block rows of a row index. The slots of one device in one panel name distinct (block row, block column) pairs. `block_cols`: block columns index the 16 block columns of a col index's part of the panel. `block_counts`: in every panel, all devices of at least one row index hold exactly 20 live blocks.
All inputs are finite; a program needn't handle non-finite values.
Results may differ from a plain program's by a relative error of at most 0.0044.
Values may be sent and summed in bfloat16 or wider, within the bound.
No kernel may reach another device: no remote copies, remote signals or barrier semaphores. Data moves between devices by JAX's collectives and lax.ppermute only.
A program may use at most 64 MiB of HBM per device.

v0:
```python
import jax
import jax.numpy as jnp
from jax import lax
from jax.sharding import Mesh
from jax.sharding import PartitionSpec as P

ROWB_DEV = 48
PCB = 16
COL = ("col_0", "col_1")
ROW_COL = ("row", "col_0", "col_1")


def in_blocks(x, dim, peers):
    before, after = (x.shape[:dim], x.shape[dim + 1 :])
    return jnp.moveaxis(x.reshape(*before, peers, -1, *after), dim, 0)


def edges_of(length, count):
    hop = length // count
    if hop >= 8:
        hop -= hop % 8
    return [hop * k for k in range(1, count)]


def in_order(tiles, dim):
    tiles = jnp.moveaxis(tiles, 0, dim)
    lengths = tiles.shape
    return tiles.reshape(*lengths[:dim], lengths[dim] * lengths[dim + 1], *lengths[dim + 2 :])


def several_exchanges(x, axis, pieces, split_dim, concat_dim):
    tiles = in_blocks(x, split_dim, lax.axis_size(axis))
    widest = max(range(1, max(2, tiles.ndim - 1)), key=lambda d: tiles.shape[d])
    finished = []
    for share in jnp.split(tiles, edges_of(tiles.shape[widest], pieces), axis=widest):
        if share.size:
            finished.append(lax.all_to_all(share, axis, split_axis=0, concat_axis=0, tiled=True))
    return in_order(jnp.concatenate(finished, axis=widest), concat_dim)


def scatter_axes(x, axes, dim):
    for axis in axes:
        x = lax.psum_scatter(x, axis, scatter_dimension=dim, tiled=True)
    return x


def spread_rows(running, values, feature_cols, row_ids, live_scale):
    contrib = jnp.einsum("bfk,brk->bfr", feature_cols, values, preferred_element_type=jnp.float32)
    return running.at[row_ids].add(contrib * live_scale[:, None, None])


def body(
    adj_values, block_rows, block_cols, block_counts, block_scales, panel_features, weight, out_bias
):
    nsteps = adj_values.shape[0]
    blocksz = adj_values.shape[4]
    feat_all = weight.shape[0]
    out_width = weight.shape[1]
    rows_here = ROWB_DEV * blocksz // lax.axis_size(COL)
    panels = lax.all_gather(panel_features, "row", axis=2, tiled=True)
    shares = several_exchanges(panels, COL, 2, 2, 1)
    share_blocks = shares.reshape(nsteps, feat_all, PCB, blocksz).transpose(0, 2, 1, 3)
    running = jnp.zeros((ROWB_DEV, feat_all, blocksz), jnp.float32)
    slot_ids = jnp.arange(adj_values.shape[3], dtype=jnp.int32)
    for step in range(nsteps):
        live_scale = jnp.where(
            slot_ids < block_counts[step, 0, 0], block_scales[step, 0, 0].astype(jnp.float32), 0.0
        )
        feature_cols = share_blocks[step][block_cols[step, 0, 0]]
        running = spread_rows(
            running, adj_values[step, 0, 0], feature_cols, block_rows[step, 0, 0], live_scale
        )
    summed = scatter_axes(running, COL, 0)
    aggregate = summed.astype(jnp.bfloat16)
    before = jnp.einsum(
        "zfr,fg->zrg", aggregate, weight, preferred_element_type=jnp.float32
    ).reshape(rows_here, out_width)
    return jax.nn.relu(before + out_bias).astype(jnp.bfloat16)


def solution(mesh):
    split = Mesh(mesh.devices.reshape(mesh.shape["row"], 8, 2), ("row", "col_0", "col_1"))
    in_specs = (
        P(None, "row", COL, None, None, None),
        P(None, "row", COL, None),
        P(None, "row", COL, None),
        P(None, "row", COL),
        P(None, "row", COL, None),
        P(None, COL, "row"),
        P(),
        P(),
    )
    out_specs = P(ROW_COL, None)
    return jax.shard_map(body, mesh=split, in_specs=in_specs, out_specs=out_specs, check_vma=False)
```

profile of v0, /device:TPU:1, one launch (start us, length us, event | category | flops | bytes accessed | tf_op | source)
XLA Modules:
  0.0 258.9 jit_solution(18103866229574193103)
XLA Ops:
  6.5 0.7 all-gather.2.cloned.1.call-update
  7.3 42.4 %all-gather.2.cloned.1.call-done = bf16[2,16,32768]{2,1,0:T(8,128)(2,1)} async-done(((bf16[2,16,2048]{2,1,0:T(8,128)(2,1)}), bf16[2,16,32768]{2,1,0:T(8,128)(2,1)}) %all-gather.2.cloned.1.call-update) | async-done | bytes 2097168 | tf_op jit(solution)/shard_map/all_gather | solution.py:60
  49.6 2.7 %copy.21 = bf16[4,8,16,2048]{3,2,1,0:T(8,128)(2,1)S(1)} copy(bf16[4,8,16,2048]{3,1,2,0:T(8,128)(2,1)} %bitcast.67) | data formatting | bytes 4194304
  52.4 0.2 bitcast_bitcast_fusion
  52.6 0.1 fusion.13
  52.8 1.6 copy.15
  54.4 8.9 %all-to-all-start = ((bf16[16,2,8,2048]{3,2,1,0:T(8,128)(2,1)}), bf16[16,2,8,2048]{3,2,1,0:T(8,128)(2,1)S(1)}, u32[]{:S(2)}, u32[]{:S(2)}) async-start(bf16[16,2,8,2048]{3,2,1,0:T(8,128)(2,1)} %copy.15), calls=%async_computation | async-start | bytes 2097152 | tf_op jit(solution)/shard_map/all_to_all | solution.py:37
  63.3 1.6 copy.16
  64.9 25.6 %all-to-all-done = bf16[16,2,8,2048]{3,2,1,0:T(8,128)(2,1)S(1)} async-done(((bf16[16,2,8,2048]{3,2,1,0:T(8,128)(2,1)}), bf16[16,2,8,2048]{3,2,1,0:T(8,128)(2,1)S(1)}, u32[]{:S(2)}, u32[]{:S(2)}) %all-to-all-start) | async-done | bytes 1048608 | tf_op jit(solution)/shard_map/all_to_all | solution.py:37
  90.5 5.9 %all-to-all-start.1 = ((bf16[16,2,8,2048]{3,2,1,0:T(8,128)(2,1)}), bf16[16,2,8,2048]{3,2,1,0:T(8,128)(2,1)S(1)}, u32[]{:S(2)}, u32[]{:S(2)}) async-start(bf16[16,2,8,2048]{3,2,1,0:T(8,128)(2,1)} %copy.16), calls=%async_computation.1 | async-start | bytes 2097152 | tf_op jit(solution)/shard_map/all_to_all | solution.py:37
  96.5 0.0 reduce-scatter.3.cloned.1.call-start
  96.5 0.6 fusion.14
  97.1 1.8 compare_select_fusion.4
  99.0 23.6 %all-to-all-done.1 = bf16[16,2,8,2048]{3,2,1,0:T(8,128)(2,1)S(1)} async-done(((bf16[16,2,8,2048]{3,2,1,0:T(8,128)(2,1)}), bf16[16,2,8,2048]{3,2,1,0:T(8,128)(2,1)S(1)}, u32[]{:S(2)}, u32[]{:S(2)}) %all-to-all-start.1) | async-done | bytes 1048608 | tf_op jit(solution)/shard_map/all_to_all | solution.py:37
  122.5 0.1 maximum_bitcast_fusion
  122.7 0.2 copy.17
  122.9 0.6 copy.22
  123.5 0.5 copy.24
  124.1 0.1 slice_bitcast_fusion
  124.2 0.8 gather_fusion
  125.1 1.9 gather_fusion.1
  127.0 3.3 %convolution_multiply_fusion.1 = f32[20,256,128]{2,1,0:T(8,128)} fusion(bf16[20,256,128]{2,1,0:T(8,128)(2,1)S(1)} %gather_fusion, f32[20]{0:T(128)S(1)} %copy-done.4, bf16[2,1,1,20,128,128]{5,4,3,2,1,0:T(8,128)(2,1)} %param.8), kind=kOutput, calls=%fused_computation.8 | convolution fusion | flops 168427520 | bytes 4587600 | tf_op jit(solution)/shard_map/bfk,brk->bfr/dot_general | solution.py:48
  130.3 0.5 convolution_multiply_fusion
  130.8 3.4 %broadcast_in_dim.7 = f32[48,256,128]{2,1,0:T(8,128)} broadcast(f32[]{:T(128)} %constant.4.clone.1), dimensions={} | broadcast | bytes 6291460 | tf_op jit(solution)/shard_map/broadcast_in_dim | solution.py:63
  134.2 9.5 %scatter_fusion = f32[48,256,128]{2,1,0:T(8,128)} fusion(f32[48,256,128]{2,1,0:T(8,128)} %broadcast_in_dim.7, s32[20]{0:T(128)S(1)} %get-tuple-element.12, f32[20,256,128]{2,1,0:T(8,128)} %convolution_multiply_fusion.1), kind=kCustom, calls=%fused_computation.2 | custom fusion | flops 655360 | bytes 7864400 | tf_op jit(solution)/shard_map/scatter-add | solution.py:49
  143.7 8.5 %scatter_fusion.1 = f32[48,256,128]{2,1,0:T(8,128)} fusion(f32[48,256,128]{2,1,0:T(8,128)} %scatter_fusion, s32[20]{0:T(128)S(1)} %get-tuple-element.11, f32[20,256,128]{2,1,0:T(8,128)S(1)} %convolution_multiply_fusion), kind=kCustom, calls=%fused_computation.3 | custom fusion | flops 655360 | bytes 7864400 | tf_op jit(solution)/shard_map/scatter-add | solution.py:49
  152.2 0.0 reduce-scatter.3.cloned.1.call-update
  152.2 0.0 reduce-scatter.5.cloned.1.call-start
  152.3 73.0 %reduce-scatter.3.cloned.1.call-done = f32[6,256,128]{2,1,0:T(8,128)} async-done(((f32[48,256,128]{2,1,0:T(8,128)}), f32[6,256,128]{2,1,0:T(8,128)}) %reduce-scatter.3.cloned.1.call-update) | async-done | bytes 786448 | tf_op jit(solution)/shard_map/reduce_scatter | solution.py:43
  225.3 25.1 %reduce-scatter.5.cloned.1.call-done = f32[3,256,128]{2,1,0:T(8,128)} async-done(((f32[6,256,128]{2,1,0:T(8,128)}), f32[3,256,128]{2,1,0:T(8,128)}) %reduce-scatter.5.cloned.1.call-update) | async-done | bytes 393232 | tf_op jit(solution)/shard_map/reduce_scatter | solution.py:43
  250.4 1.2 fusion.6
  251.7 0.7 fusion.5
  (25 shorter events, 0.1 us)
Async XLA Ops:
  6.5 243.9 %copy-start = (bf16[256,256]{1,0:T(8,128)(2,1)S(1)}, bf16[256,256]{1,0:T(8,128)(2,1)}, u32[]{:S(2)}) copy-start(bf16[256,256]{1,0:T(8,128)(2,1)} %param.14) | copy-start | bytes 393220
  6.5 43.1 %all-gather.2.cloned.1.call-start = ((), (), s32[]{:S(2)}) async-start(), calls=%async_computation.4 | async-start | bytes 2228224 | tf_op jit(solution)/shard_map/all_gather | solution.py:60
  54.4 36.2 %all-to-all-start = ((bf16[16,2,8,2048]{3,2,1,0:T(8,128)(2,1)}), bf16[16,2,8,2048]{3,2,1,0:T(8,128)(2,1)S(1)}, u32[]{:S(2)}, u32[]{:S(2)}) async-start(bf16[16,2,8,2048]{3,2,1,0:T(8,128)(2,1)} %copy.15), calls=%async_computation | async-start | bytes 2097152 | tf_op jit(solution)/shard_map/all_to_all | solution.py:37
  63.3 33.2 %copy-start.6 = (s32[2,1,1]{0,2,1:T(1,128)S(1)}, s32[2,1,1]{0,2,1:T(1,128)}, u32[]{:S(2)}) copy-start(s32[2,1,1]{0,2,1:T(1,128)} %param.11) | copy-start | bytes 28
  63.3 33.8 %copy-start.8 = (s32[2,1,1,20]{3,2,1,0:T(1,128)S(1)}, s32[2,1,1,20]{3,2,1,0:T(1,128)}, u32[]{:S(2)}) copy-start(s32[2,1,1,20]{3,2,1,0:T(1,128)} %param.10) | copy-start | bytes 484
  63.3 33.8 %copy-start.9 = (s32[2,1,1,20]{3,2,1,0:T(1,128)S(1)}, s32[2,1,1,20]{3,2,1,0:T(1,128)}, u32[]{:S(2)}) copy-start(s32[2,1,1,20]{3,2,1,0:T(1,128)} %param.9) | copy-start | bytes 484
  63.3 33.8 %copy-start.5 = (bf16[2,1,1,20]{3,0,2,1:T(2,128)(2,1)S(1)}, bf16[2,1,1,20]{3,0,2,1:T(2,128)(2,1)}, u32[]{:S(2)}) copy-start(bf16[2,1,1,20]{3,0,2,1:T(2,128)(2,1)} %param.12) | copy-start | bytes 244
  90.5 32.0 %all-to-all-start.1 = ((bf16[16,2,8,2048]{3,2,1,0:T(8,128)(2,1)}), bf16[16,2,8,2048]{3,2,1,0:T(8,128)(2,1)S(1)}, u32[]{:S(2)}, u32[]{:S(2)}) async-start(bf16[16,2,8,2048]{3,2,1,0:T(8,128)(2,1)} %copy.16), calls=%async_computation.1 | async-start | bytes 2097152 | tf_op jit(solution)/shard_map/all_to_all | solution.py:37
  96.5 128.8 %reduce-scatter.3.cloned.1.call-start = ((), (), s32[]{:S(2)}) async-start(), calls=%async_computation.5 | async-start | bytes 7077888 | tf_op jit(solution)/shard_map/reduce_scatter | solution.py:43
  125.0 1.9 copy-start.4
  126.9 3.3 %copy-start.1 = (bf16[20,256,128]{2,1,0:T(8,128)(2,1)S(1)}, bf16[20,256,128]{2,1,0:T(8,128)(2,1)}, u32[]{:S(2)}) copy-start(bf16[20,256,128]{2,1,0:T(8,128)(2,1)} %gather_fusion.1) | copy-start | bytes 3932164
  126.9 3.3 %copy-start.2 = (bf16[2,1,1,20,128,128]{5,4,3,2,1,0:T(8,128)(2,1)S(1)}, bf16[2,1,1,20,128,128]{5,4,3,2,1,0:T(8,128)(2,1)}, u32[]{:S(2)}) copy-start(bf16[2,1,1,20,128,128]{5,4,3,2,1,0:T(8,128)(2,1)} %param.8) | copy-start | bytes 3932164
  127.0 3.3 %copy-start.3 = (f32[20]{0:T(128)S(1)}, f32[20]{0:T(128)}, u32[]{:S(2)}) copy-start(f32[20]{0:T(128)} %get-tuple-element.13) | copy-start | bytes 244
  152.2 99.4 %copy-start.7 = (f32[256]{0:T(256)S(1)}, f32[256]{0:T(256)}, u32[]{:S(2)}) copy-start(f32[256]{0:T(256)} %param.15) | copy-start | bytes 3076
  152.2 98.2 %reduce-scatter.5.cloned.1.call-start = ((), (), s32[]{:S(2)}) async-start(), calls=%async_computation.6 | async-start | bytes 1179648 | tf_op jit(solution)/shard_map/reduce_scatter | solution.py:43
Sparse Core Ops, SparseCore 0:
  9.1 40.4 all-gather.1
  152.4 72.8 reduce-scatter.2
  227.7 22.5 reduce-scatter.4
where the time goes:
time: 259 us
  waiting for transfers between devices  190 us (73%)
  other arithmetic  20.7 us (8%)
  starting transfers between devices  14.9 us (6%)
  local copies, waits for them, and re-layouts  14.5 us (6%)
  between operations  13.3 us (5%)
  matrix products  5.03 us (2%)
    reduce_scatter x2, waiting for transfers between devices, scatter_axes(): x = lax.psum_scatter(x, axis, scatter_dimension=dim, tiled=True)  98.1 us
    all_to_all x2, waiting for transfers between devices, several_exchanges(): lax.all_to_all(share, axis, split_axis=0, concat_axis=0, tiled=True)  49.2 us
    all_gather x1, waiting for transfers between devices, body(): panels = lax.all_gather(panel_features, 'row', axis=2, tiled=True)  42.4 us
    scatter-add x2, other arithmetic, spread_rows(): return running.at[row_ids].add(contrib * live_scale[:, None, None])  18 us
    all_to_all x2, starting transfers between devices, several_exchanges(): lax.all_to_all(share, axis, split_axis=0, concat_axis=0, tiled=True)  14.8 us
  transfers between devices with their start and end apart: 5, of which 5 were waited for; matrix products, arithmetic and copies ran while one was open for 2% of the time, Pallas kernels for 0%

commit v1 on v0

--- a/solution.py
+++ b/solution.py
@@ -57,7 +57,9 @@
     feat_all = weight.shape[0]
     out_width = weight.shape[1]
     rows_here = ROWB_DEV * blocksz // lax.axis_size(COL)
-    panels = lax.all_gather(panel_features, "row", axis=2, tiled=True)
+    panels = jnp.concatenate(
+        lax.all_to_all(jnp.stack([panel_features] * lax.axis_size("row")), "row", 0, 0), axis=2
+    )
     shares = several_exchanges(panels, COL, 2, 2, 1)
     share_blocks = shares.reshape(nsteps, feat_all, PCB, blocksz).transpose(0, 2, 1, 3)
     running = jnp.zeros((ROWB_DEV, feat_all, blocksz), jnp.float32)

time: 259 us -> 249 us (0.961)
  blocking collectives: 0 us -> 71.7 us
  waiting for transfers between devices: 190 us -> 123 us
  starting transfers between devices: 14.9 us -> 4.4 us
  local copies, waits for them, and re-layouts: 14.5 us -> 10.6 us
    all_to_all x0 -> x2, blocking collectives: none -> 71.7 us  [the longest x1 38.5 us: several_exchanges(): lax.all_to_all(share, axis, split_axis=0, concat_axis=0, tiled=True)]
    all_gather x1 -> x0, waiting for transfers between devices: 42.4 us -> none  [body(): panels = lax.all_gather(panel_features, 'row', axis=2, tiled=True)]
    all_to_all x2 -> x1, waiting for transfers between devices: 49.2 us -> 23.6 us  [several_exchanges(): lax.all_to_all(share, axis, split_axis=0, concat_axis=0, tiled=True)]
    all_to_all x2 -> x1, starting transfers between devices: 14.8 us -> 4.32 us  [several_exchanges(): lax.all_to_all(share, axis, split_axis=0, concat_axis=0, tiled=True)]
    unnamed x22 -> x21, local copies, waits for them, and re-layouts: 3.42 us -> 0.67 us
  transfers between devices with their start and end apart: 5 -> 3, of which waited for: 5 -> 3; matrix products, arithmetic and copies ran while one was open for 2% -> 1% of each run, Pallas kernels for 0% -> 0%
where the time goes in v1:
time: 249 us; the launch traced here: 248 us
  waiting for transfers between devices  123 us (49%)
  blocking collectives  71.7 us (29%)
  other arithmetic  20.4 us (8%)
  between operations  13.6 us (5%)
  local copies, waits for them, and re-layouts  10.6 us (4%)
  matrix products  5.04 us (2%)
  starting transfers between devices  4.4 us (2%)
    reduce_scatter x2, waiting for transfers between devices, scatter_axes(): x = lax.psum_scatter(x, axis, scatter_dimension=dim, tiled=True)  98.9 us
    all_to_all x1, blocking collectives, several_exchanges(): lax.all_to_all(share, axis, split_axis=0, concat_axis=0, tiled=True)  38.5 us
    all_to_all x1, blocking collectives, body(): lax.all_to_all(jnp.stack([panel_features] * lax.axis_size('row')), 'row',...  33.2 us
    all_to_all x1, waiting for transfers between devices, several_exchanges(): lax.all_to_all(share, axis, split_axis=0, concat_axis=0, tiled=True)  23.6 us
    scatter-add x2, other arithmetic, spread_rows(): return running.at[row_ids].add(contrib * live_scale[:, None, None])  17.8 us
  transfers between devices with their start and end apart: 3, of which 3 were waited for; matrix products, arithmetic and copies ran while one was open for 1% of the time, Pallas kernels for 0%

profile of v1, /device:TPU:1, one launch (start us, length us, event | category | flops | bytes accessed | tf_op | source)
XLA Modules:
  0.0 248.2 jit_solution(5152177760272052376)
XLA Ops:
  6.5 0.0 copy-start
  6.5 1.2 stack.2
  7.7 33.2 %all_to_all.15 = bf16[16,2,16,2048]{3,2,1,0:T(8,128)(2,1)S(1)} all-to-all(bf16[16,2,16,2048]{3,2,1,0:T(8,128)(2,1)S(1)} %stack.2), channel_id=1, replica_groups=mesh['row'=16,'col_0'=8,'col_1'=2] {'row'}, dimensions={0} | all-to-all | bytes 4194304 | tf_op jit(solution)/shard_map/all_to_all | solution.py:61
  40.9 1.2 fusion.13
  42.1 38.5 %all_to_all.16 = bf16[16,2,8,2048]{3,2,1,0:T(8,128)(2,1)S(1)} all-to-all(bf16[16,2,8,2048]{3,2,1,0:T(8,128)(2,1)S(1)} %get-tuple-element.7), channel_id=1, replica_groups=mesh['row'=16,'col_0'=8,'col_1'=2] {'col_0','col_1'}, dimensions={0} | all-to-all | bytes 2097152 | tf_op jit(solution)/shard_map/all_to_all | solution.py:37
  80.6 4.3 %all-to-all-start.2 = ((bf16[16,2,8,2048]{3,2,1,0:T(8,128)(2,1)}), bf16[16,2,8,2048]{3,2,1,0:T(8,128)(2,1)S(1)}, u32[]{:S(2)}, u32[]{:S(2)}) async-start(bf16[16,2,8,2048]{3,2,1,0:T(8,128)(2,1)} %get-tuple-element.8), calls=%async_computation.2 | async-start | bytes 2097152 | tf_op jit(solution)/shard_map/all_to_all | solution.py:37
  84.9 0.0 reduce-scatter.3.cloned.1.call-start
  85.0 0.6 fusion.14
  85.6 1.7 compare_select_fusion.4
  87.4 23.6 %all-to-all-done.2 = bf16[16,2,8,2048]{3,2,1,0:T(8,128)(2,1)S(1)} async-done(((bf16[16,2,8,2048]{3,2,1,0:T(8,128)(2,1)}), bf16[16,2,8,2048]{3,2,1,0:T(8,128)(2,1)S(1)}, u32[]{:S(2)}, u32[]{:S(2)}) %all-to-all-start.2) | async-done | bytes 1048608 | tf_op jit(solution)/shard_map/all_to_all | solution.py:37
  110.9 0.1 maximum_bitcast_fusion
  111.1 0.2 copy.11
  111.3 0.6 copy.15
  112.0 0.5 copy.17
  112.5 0.1 slice_bitcast_fusion
  112.7 0.8 gather_fusion
  113.5 0.0 copy-start.4
  113.5 1.9 gather_fusion.1
  115.4 3.3 %convolution_multiply_fusion.1 = f32[20,256,128]{2,1,0:T(8,128)} fusion(bf16[20,256,128]{2,1,0:T(8,128)(2,1)S(1)} %gather_fusion, f32[20]{0:T(128)S(1)} %copy-done.4, bf16[2,1,1,20,128,128]{5,4,3,2,1,0:T(8,128)(2,1)} %param.8), kind=kOutput, calls=%fused_computation.7 | convolution fusion | flops 168427520 | bytes 4587600 | tf_op jit(solution)/shard_map/bfk,brk->bfr/dot_general | solution.py:48
  118.7 0.0 copy-done.2
  118.7 0.5 convolution_multiply_fusion
  119.2 3.4 %broadcast_in_dim.7 = f32[48,256,128]{2,1,0:T(8,128)} broadcast(f32[]{:T(128)} %constant.4.clone.1), dimensions={} | broadcast | bytes 6291460 | tf_op jit(solution)/shard_map/broadcast_in_dim | solution.py:65
  122.6 9.3 %scatter_fusion = f32[48,256,128]{2,1,0:T(8,128)} fusion(f32[48,256,128]{2,1,0:T(8,128)} %broadcast_in_dim.7, s32[20]{0:T(128)S(1)} %get-tuple-element.12, f32[20,256,128]{2,1,0:T(8,128)} %convolution_multiply_fusion.1), kind=kCustom, calls=%fused_computation.2 | custom fusion | flops 655360 | bytes 7864400 | tf_op jit(solution)/shard_map/scatter-add | solution.py:49
  131.9 8.5 %scatter_fusion.1 = f32[48,256,128]{2,1,0:T(8,128)} fusion(f32[48,256,128]{2,1,0:T(8,128)} %scatter_fusion, s32[20]{0:T(128)S(1)} %get-tuple-element.11, f32[20,256,128]{2,1,0:T(8,128)S(1)} %convolution_multiply_fusion), kind=kCustom, calls=%fused_computation.3 | custom fusion | flops 655360 | bytes 7864400 | tf_op jit(solution)/shard_map/scatter-add | solution.py:49
  140.4 0.0 reduce-scatter.3.cloned.1.call-update
  140.4 0.0 reduce-scatter.5.cloned.1.call-start
  140.5 73.8 %reduce-scatter.3.cloned.1.call-done = f32[6,256,128]{2,1,0:T(8,128)} async-done(((f32[48,256,128]{2,1,0:T(8,128)}), f32[6,256,128]{2,1,0:T(8,128)}) %reduce-scatter.3.cloned.1.call-update) | async-done | bytes 786448 | tf_op jit(solution)/shard_map/reduce_scatter | solution.py:43
  214.3 0.0 reduce-scatter.5.cloned.1.call-update
  214.3 25.1 %reduce-scatter.5.cloned.1.call-done = f32[3,256,128]{2,1,0:T(8,128)} async-done(((f32[6,256,128]{2,1,0:T(8,128)}), f32[3,256,128]{2,1,0:T(8,128)}) %reduce-scatter.5.cloned.1.call-update) | async-done | bytes 393232 | tf_op jit(solution)/shard_map/reduce_scatter | solution.py:43
  239.4 1.2 fusion.6
  240.7 0.0 copy-done.7
  240.7 0.7 fusion.5
  (19 shorter events, 0.0 us)
Async XLA Ops:
  6.5 232.9 %copy-start = (bf16[256,256]{1,0:T(8,128)(2,1)S(1)}, bf16[256,256]{1,0:T(8,128)(2,1)}, u32[]{:S(2)}) copy-start(bf16[256,256]{1,0:T(8,128)(2,1)} %param.14) | copy-start | bytes 393220
  42.1 42.9 %copy-start.6 = (s32[2,1,1]{0,2,1:T(1,128)S(1)}, s32[2,1,1]{0,2,1:T(1,128)}, u32[]{:S(2)}) copy-start(s32[2,1,1]{0,2,1:T(1,128)} %param.11) | copy-start | bytes 28
  42.1 43.5 %copy-start.8 = (s32[2,1,1,20]{3,2,1,0:T(1,128)S(1)}, s32[2,1,1,20]{3,2,1,0:T(1,128)}, u32[]{:S(2)}) copy-start(s32[2,1,1,20]{3,2,1,0:T(1,128)} %param.10) | copy-start | bytes 484
  42.1 43.5 %copy-start.9 = (s32[2,1,1,20]{3,2,1,0:T(1,128)S(1)}, s32[2,1,1,20]{3,2,1,0:T(1,128)}, u32[]{:S(2)}) copy-start(s32[2,1,1,20]{3,2,1,0:T(1,128)} %param.9) | copy-start | bytes 484
  42.1 43.5 %copy-start.5 = (bf16[2,1,1,20]{3,0,2,1:T(2,128)(2,1)S(1)}, bf16[2,1,1,20]{3,0,2,1:T(2,128)(2,1)}, u32[]{:S(2)}) copy-start(bf16[2,1,1,20]{3,0,2,1:T(2,128)(2,1)} %param.12) | copy-start | bytes 244
  80.6 30.3 %all-to-all-start.2 = ((bf16[16,2,8,2048]{3,2,1,0:T(8,128)(2,1)}), bf16[16,2,8,2048]{3,2,1,0:T(8,128)(2,1)S(1)}, u32[]{:S(2)}, u32[]{:S(2)}) async-start(bf16[16,2,8,2048]{3,2,1,0:T(8,128)(2,1)} %get-tuple-element.8), calls=%async_computation.2 | async-start | bytes 2097152 | tf_op jit(solution)/shard_map/all_to_all | solution.py:37
  84.9 129.3 %reduce-scatter.3.cloned.1.call-start = ((), (), s32[]{:S(2)}) async-start(), calls=%async_computation.5 | async-start | bytes 7077888 | tf_op jit(solution)/shard_map/reduce_scatter | solution.py:43
  113.5 1.9 copy-start.4
  115.3 3.3 %copy-start.1 = (bf16[20,256,128]{2,1,0:T(8,128)(2,1)S(1)}, bf16[20,256,128]{2,1,0:T(8,128)(2,1)}, u32[]{:S(2)}) copy-start(bf16[20,256,128]{2,1,0:T(8,128)(2,1)} %gather_fusion.1) | copy-start | bytes 3932164
  115.3 3.3 %copy-start.2 = (bf16[2,1,1,20,128,128]{5,4,3,2,1,0:T(8,128)(2,1)S(1)}, bf16[2,1,1,20,128,128]{5,4,3,2,1,0:T(8,128)(2,1)}, u32[]{:S(2)}) copy-start(bf16[2,1,1,20,128,128]{5,4,3,2,1,0:T(8,128)(2,1)} %param.8) | copy-start | bytes 3932164
  115.3 3.3 %copy-start.3 = (f32[20]{0:T(128)S(1)}, f32[20]{0:T(128)}, u32[]{:S(2)}) copy-start(f32[20]{0:T(128)} %get-tuple-element.13) | copy-start | bytes 244
  140.4 100.3 %copy-start.7 = (f32[256]{0:T(256)S(1)}, f32[256]{0:T(256)}, u32[]{:S(2)}) copy-start(f32[256]{0:T(256)} %param.15) | copy-start | bytes 3076
  140.4 99.0 %reduce-scatter.5.cloned.1.call-start = ((), (), s32[]{:S(2)}) async-start(), calls=%async_computation.6 | async-start | bytes 1179648 | tf_op jit(solution)/shard_map/reduce_scatter | solution.py:43
Sparse Core Ops, SparseCore 0:
  140.5 73.6 reduce-scatter.2
  216.8 22.5 reduce-scatter.4
